TPU v7x, 32 devices: a whole 2x2x4 slice. The times are simulated.
32 devices in a mesh: fsdp: 4 (over y, x), ctx: 4 (over z), tp: 2 (over core).
Axes of the slice: x: 2, y: 2, z: 4, core: 2. Of those that a mesh axis runs over, the one named last changes fastest.
Arguments:
- tokens: bfloat16 [4, 2048, 1024], P('fsdp', 'ctx'), may hold values from -6 to 6
- segment_ids: int32 [4, 2048], P('fsdp', 'ctx'), may hold values from 0 to 10, as said below
- positions: int32 [4, 2048], P('fsdp', 'ctx'), may hold values from 0 to 2047, as said below
- attention_gain: bfloat16 [1024], P('fsdp'), may hold values from 0.099609375 to 1.8984375
- attention_shift: bfloat16 [1024], P('fsdp'), may hold values from -1.75 to 1.75
- feedforward_gain: bfloat16 [1024], P('fsdp'), may hold values from 0.099609375 to 1.8984375
- feedforward_shift: bfloat16 [1024], P('fsdp'), may hold values from -1.75 to 1.75
- joint_weight: bfloat16 [1024, 3, 1024], P('fsdp', None, 'tp'), may hold values from -8 to 8
- joint_bias: bfloat16 [3, 1024], P(None, ('tp', 'fsdp')), may hold values from -3 to 3
- output_weight: bfloat16 [1024, 1024], P('tp', 'fsdp'), may hold values from -1.5 to 1.5
- output_bias: bfloat16 [1024], P('fsdp'), may hold values from -1.75 to 1.75
- up_weight: bfloat16 [1024, 4096], P('fsdp', 'tp'), may hold values from -0.1875 to 0.1875
- up_bias: bfloat16 [4096], P(('tp', 'fsdp')), may hold values from -3 to 3
- down_weight: bfloat16 [4096, 1024], P('tp', 'fsdp'), may hold values from -0.09375 to 0.09375
- down_bias: bfloat16 [1024], P('fsdp'), may hold values from -1.75 to 1.75
- cotangent: float32 [4, 2048, 1024], P('fsdp', 'ctx'), may hold values from -6 to 6
Outputs:
- result: float32 [4, 2048, 1024], P('fsdp', 'ctx')
- tokens_grad: float32 [4, 2048, 1024], P('fsdp', 'ctx')
- attention_gain_grad: float32 [1024], P('fsdp')
- attention_shift_grad: float32 [1024], P('fsdp')
- feedforward_gain_grad: float32 [1024], P('fsdp')
- feedforward_shift_grad: float32 [1024], P('fsdp')
- joint_weight_grad: float32 [1024, 3, 1024], P('fsdp', None, 'tp')
- joint_bias_grad: float32 [3, 1024], P(None, ('tp', 'fsdp'))
- output_weight_grad: float32 [1024, 1024], P('tp', 'fsdp')
- output_bias_grad: float32 [1024], P('fsdp')
- up_weight_grad: float32 [1024, 4096], P('fsdp', 'tp')
- up_bias_grad: float32 [4096], P(('tp', 'fsdp'))
- down_weight_grad: float32 [4096, 1024], P('tp', 'fsdp')
- down_bias_grad: float32 [1024], P('fsdp')
Inputs may be any that keep to these rules, and one draw needn't show every extreme that they name: `segment_ids`: along each sequence the ids start at 0 and rise by one at each document's first token; a document holds 204 to 2048 tokens, the last one cut at the sequence's end. The first sequence is one document; the last sequence is documents of 204 tokens. `positions`: each token's offset from the first token of its document; the first sequence is one document.
All inputs are finite; a program needn't handle non-finite values.
Results may differ from a plain program's by a relative error of at most 0.011.
Values may be sent and summed in bfloat16 or wider, within the bound.
No kernel may reach another device: no remote copies, remote signals or barrier semaphores. Data moves between devices by JAX's collectives and lax.ppermute only.
A program may use at most 192 MiB of HBM per device.

v0:
```python
import jax
import jax.numpy as jnp
from jax import lax
from jax.sharding import PartitionSpec as P

HD = 64
ROT = 16
EPS = 1e-05
ROPE_BASE = 10000.0


def rope_tables(offsets):
    half_dim = ROT // 2
    freq = ROPE_BASE ** (-(jnp.arange(half_dim, dtype=jnp.float32) * 2.0 / ROT))
    angle = offsets.astype(jnp.float32)[:, None] * freq[None, :]
    return (jnp.cos(angle)[:, None, :], jnp.sin(angle)[:, None, :])


def rotate(tensor, cosine, sine):
    half_dim = ROT // 2
    front = tensor[..., :half_dim]
    middle = tensor[..., half_dim:ROT]
    return jnp.concatenate(
        [front * cosine - middle * sine, middle * cosine + front * sine, tensor[..., ROT:]], axis=-1
    )


def unrotate(grads, cosine, sine):
    half_dim = ROT // 2
    front = grads[..., :half_dim]
    middle = grads[..., half_dim:ROT]
    return jnp.concatenate(
        [front * cosine + middle * sine, middle * cosine - front * sine, grads[..., ROT:]], axis=-1
    )


def normalize(rows):
    center = jnp.mean(rows, -1, keepdims=True)
    centred = rows - center
    spread = jnp.mean(centred * centred, -1, keepdims=True)
    rstd = lax.rsqrt(spread + EPS)
    return (centred * rstd, rstd)


def norm_back(upstream, normed, rstd, gain):
    scaled = upstream * gain
    return rstd * (
        scaled
        - jnp.mean(scaled, -1, keepdims=True)
        - normed * jnp.mean(scaled * normed, -1, keepdims=True)
    )


def masked_scores(query_blk, query_index, query_seg, keys, key_seg):
    scores = jnp.einsum(
        "qhe,khe->hqk", query_blk, keys, preferred_element_type=jnp.float32
    ) * HD ** (-0.5)
    key_index = jnp.arange(keys.shape[0], dtype=jnp.int32)
    allowed = (key_seg[None, :] == query_seg[:, None]) & (
        key_index[None, :] <= query_index[:, None]
    )
    return jnp.where(allowed[None], scores, -jnp.inf)


def local(
    tokens,
    segment_ids,
    positions,
    attention_gain,
    attention_shift,
    feedforward_gain,
    feedforward_shift,
    joint_weight,
    joint_bias,
    output_weight,
    output_bias,
    up_weight,
    up_bias,
    down_weight,
    down_bias,
    cotangent,
):
    f32 = jnp.float32
    bf16 = jnp.bfloat16
    scale = HD ** (-0.5)
    small = jnp.stack(
        [
            attention_gain,
            attention_shift,
            feedforward_gain,
            feedforward_shift,
            output_bias,
            down_bias,
        ]
    )
    full_joint, full_output, full_up, full_down, full_small, full_jbias, full_upbias = (
        lax.all_gather(joint_weight, "fsdp", axis=0, tiled=True),
        lax.all_gather(output_weight, "fsdp", axis=1, tiled=True),
        lax.all_gather(up_weight, "fsdp", axis=0, tiled=True),
        lax.all_gather(down_weight, "fsdp", axis=1, tiled=True),
        lax.all_gather(small, "fsdp", axis=1, tiled=True),
        lax.all_gather(joint_bias, "fsdp", axis=1, tiled=True),
        lax.all_gather(up_bias, "fsdp", axis=0, tiled=True),
    )
    params = full_small.astype(f32)
    gain_one = params[0]
    shift_one = params[1]
    gain_two = params[2]
    shift_two = params[3]
    rows = tokens[0].astype(f32)
    count_rows = rows.shape[0]
    local_width = joint_weight.shape[2]
    heads_here = local_width // HD
    normed, rstd = normalize(rows)
    first = (normed * gain_one + shift_one).astype(bf16)
    second = (normed * gain_two + shift_two).astype(bf16)
    joint = (
        jnp.einsum("nd,dpe->npe", first, full_joint, preferred_element_type=f32)
        + full_jbias.astype(f32)[None]
    )
    cosine, sine = rope_tables(positions[0])
    queries = rotate(joint[:, 0].reshape(count_rows, heads_here, HD), cosine, sine).astype(bf16)
    keys_here = rotate(joint[:, 1].reshape(count_rows, heads_here, HD), cosine, sine).astype(bf16)
    values_here = joint[:, 2].reshape(count_rows, heads_here, HD).astype(bf16)
    seg_here = segment_ids[0]
    all_keys, all_values, all_segs = (
        lax.all_gather(keys_here, "ctx", axis=0, tiled=True),
        lax.all_gather(values_here, "ctx", axis=0, tiled=True),
        lax.all_gather(seg_here.astype(bf16), "ctx", axis=0, tiled=True),
    )
    key_seg = all_segs.astype(f32)
    query_seg = seg_here.astype(f32)
    query_index = lax.axis_index("ctx") * count_rows + jnp.arange(count_rows, dtype=jnp.int32)
    block = min(512, count_rows)
    count_blocks = count_rows // block
    query_blocks = queries.reshape(count_blocks, block, heads_here, HD)
    index_blocks = query_index.reshape(count_blocks, block)
    seg_blocks = query_seg.reshape(count_blocks, block)

    def forward_block(args):
        query_blk, block_index, block_seg = args
        scores = masked_scores(query_blk, block_index, block_seg, all_keys, key_seg)
        top = jnp.max(scores, -1, keepdims=True)
        lse = top + jnp.log(jnp.sum(jnp.exp(scores - top), -1, keepdims=True))
        probs = jnp.exp(scores - lse).astype(bf16)
        mixed = jnp.einsum("hqk,khe->qhe", probs, all_values, preferred_element_type=f32)
        return (mixed, lse[..., 0])

    context32, lse_all = lax.map(forward_block, (query_blocks, index_blocks, seg_blocks))
    context32 = context32.reshape(count_rows, local_width)
    context = context32.astype(bf16)
    upper = jnp.dot(second, full_up, preferred_element_type=f32) + full_upbias.astype(f32)
    activated = jax.nn.gelu(upper, approximate=False).astype(bf16)
    partial_value = jnp.dot(context, full_output, preferred_element_type=f32) + jnp.dot(
        activated, full_down, preferred_element_type=f32
    )
    mixed_all = lax.psum(partial_value, "tp")
    result = rows + mixed_all + params[4] + params[5]
    back_joint, back_output, back_up, back_down = (
        lax.all_gather(joint_weight, "fsdp", axis=0, tiled=True),
        lax.all_gather(output_weight, "fsdp", axis=1, tiled=True),
        lax.all_gather(up_weight, "fsdp", axis=0, tiled=True),
        lax.all_gather(down_weight, "fsdp", axis=1, tiled=True),
    )
    cot = cotangent[0]
    cot_b = cot.astype(bf16)
    grad_output_w = jnp.dot(context.T, cot_b, preferred_element_type=f32)
    bias_sum = jnp.sum(cot, 0)
    grad_down_w = jnp.dot(activated.T, cot_b, preferred_element_type=f32)
    d_act = jnp.einsum("nd,fd->nf", cot_b, back_down, preferred_element_type=f32)
    unused, gelu_back = jax.vjp(lambda value: jax.nn.gelu(value, approximate=False), upper)
    d_upper = gelu_back(d_act)[0]
    d_upper_b = d_upper.astype(bf16)
    grad_up_w = jnp.dot(second.T, d_upper_b, preferred_element_type=f32)
    grad_up_b = jnp.sum(d_upper, 0)
    d_second_part = jnp.einsum("nf,df->nd", d_upper_b, back_up, preferred_element_type=f32)
    d_context = (
        jnp.einsum("nd,wd->nw", cot_b, back_output, preferred_element_type=f32)
        .astype(bf16)
        .reshape(count_rows, heads_here, HD)
    )
    delta = jnp.sum(d_context.astype(f32) * context32.reshape(count_rows, heads_here, HD), -1)
    dctx_blocks = d_context.reshape(count_blocks, block, heads_here, HD)

    def backward_block(args):
        query_blk, block_index, block_seg, dctx_blk, delta_blk, lse_blk = args
        scores = masked_scores(query_blk, block_index, block_seg, all_keys, key_seg)
        probs = jnp.exp(scores - lse_blk[..., None]).astype(bf16)
        d_probs = jnp.einsum("qhe,khe->hqk", dctx_blk, all_values, preferred_element_type=f32)
        d_scores = (probs.astype(f32) * (d_probs - jnp.transpose(delta_blk)[..., None])).astype(
            bf16
        )
        d_query_blk = (
            jnp.einsum("hqk,khe->qhe", d_scores, all_keys, preferred_element_type=f32) * scale
        )
        return (probs, d_scores, d_query_blk)

    probs_all, dscores_all, d_queries = lax.map(
        backward_block,
        (
            query_blocks,
            index_blocks,
            seg_blocks,
            dctx_blocks,
            delta.reshape(count_blocks, block, heads_here),
            lse_all,
        ),
    )
    d_queries = d_queries.reshape(count_rows, heads_here, HD)
    key_part = (
        jnp.einsum("bhqk,bqhe->khe", dscores_all, query_blocks, preferred_element_type=f32) * scale
    )
    value_part = jnp.einsum("bhqk,bqhe->khe", probs_all, dctx_blocks, preferred_element_type=f32)
    key_value = lax.psum_scatter(
        jnp.concatenate(
            [
                key_part.reshape(count_rows * lax.axis_size("ctx"), local_width),
                value_part.reshape(count_rows * lax.axis_size("ctx"), local_width),
            ],
            axis=1,
        ),
        "ctx",
        scatter_dimension=0,
        tiled=True,
    )
    d_keys = key_value[:, :local_width].reshape(count_rows, heads_here, HD)
    d_values = key_value[:, local_width:]
    d_joint = jnp.stack(
        [
            unrotate(d_queries, cosine, sine).reshape(count_rows, local_width),
            unrotate(d_keys, cosine, sine).reshape(count_rows, local_width),
            d_values,
        ],
        axis=1,
    )
    d_joint_b = d_joint.astype(bf16)
    grad_joint_w = jnp.einsum("nd,npe->dpe", first, d_joint_b, preferred_element_type=f32)
    grad_joint_b = jnp.sum(d_joint, 0)
    d_first_part = jnp.einsum("npe,dpe->nd", d_joint_b, back_joint, preferred_element_type=f32)
    d_first, d_second = lax.psum((d_first_part, d_second_part), "tp")
    norm_stats = jnp.stack(
        [
            jnp.sum(d_first * normed, 0),
            jnp.sum(d_first, 0),
            jnp.sum(d_second * normed, 0),
            jnp.sum(d_second, 0),
        ]
    )
    tokens_grad = (
        cot
        + norm_back(d_first, normed, rstd, gain_one)
        + norm_back(d_second, normed, rstd, gain_two)
    )
    grad_small = jnp.concatenate([norm_stats, bias_sum[None], bias_sum[None]], axis=0)
    share_joint, share_output, share_up, share_down, share_small, share_jbias, share_upbias = (
        lax.psum_scatter(grad_joint_w, ("fsdp", "ctx"), scatter_dimension=0, tiled=True),
        lax.psum_scatter(grad_output_w, ("fsdp", "ctx"), scatter_dimension=1, tiled=True),
        lax.psum_scatter(grad_up_w, ("fsdp", "ctx"), scatter_dimension=0, tiled=True),
        lax.psum_scatter(grad_down_w, ("fsdp", "ctx"), scatter_dimension=1, tiled=True),
        lax.psum_scatter(grad_small, ("fsdp", "ctx"), scatter_dimension=1, tiled=True),
        lax.psum_scatter(grad_joint_b, ("fsdp", "ctx"), scatter_dimension=1, tiled=True),
        lax.psum_scatter(grad_up_b, ("fsdp", "ctx"), scatter_dimension=0, tiled=True),
    )
    owned = (
        lax.all_gather(share_joint, "ctx", axis=0, tiled=True),
        lax.all_gather(share_output, "ctx", axis=1, tiled=True),
        lax.all_gather(share_up, "ctx", axis=0, tiled=True),
        lax.all_gather(share_down, "ctx", axis=1, tiled=True),
        lax.all_gather(share_small, "ctx", axis=1, tiled=True),
        lax.all_gather(share_jbias, "ctx", axis=1, tiled=True),
        lax.all_gather(share_upbias, "ctx", axis=0, tiled=True),
    )
    owned_joint, owned_output, owned_up, owned_down, owned_small, owned_jbias, owned_upbias = owned
    return (
        result[None],
        tokens_grad[None],
        owned_small[0],
        owned_small[1],
        owned_small[2],
        owned_small[3],
        owned_joint,
        owned_jbias,
        owned_output,
        owned_small[4],
        owned_up,
        owned_upbias,
        owned_down,
        owned_small[5],
    )


def solution(mesh):
    placed = (
        P("fsdp", "ctx", None),
        P("fsdp", "ctx"),
        P("fsdp", "ctx"),
        P("fsdp"),
        P("fsdp"),
        P("fsdp"),
        P("fsdp"),
        P("fsdp", None, "tp"),
        P(None, ("tp", "fsdp")),
        P("tp", "fsdp"),
        P("fsdp"),
        P("fsdp", "tp"),
        P(("tp", "fsdp")),
        P("tp", "fsdp"),
        P("fsdp"),
        P("fsdp", "ctx", None),
    )
    return jax.shard_map(
        local,
        mesh=mesh,
        in_specs=placed,
        out_specs=(
            P("fsdp", "ctx", None),
            P("fsdp", "ctx", None),
            P("fsdp"),
            P("fsdp"),
            P("fsdp"),
            P("fsdp"),
            P("fsdp", None, "tp"),
            P(None, ("tp", "fsdp")),
            P("tp", "fsdp"),
            P("fsdp"),
            P("fsdp", "tp"),
            P(("tp", "fsdp")),
            P("tp", "fsdp"),
            P("fsdp"),
        ),
        check_vma=False,
    )
```

profile of v0, /device:TPU:0, one launch (start us, length us, event | category | flops | bytes accessed | tf_op | source)
XLA Modules:
  0.0 1352.6 jit_solution(17469226401049093940)
XLA Ops:
  7.3 2.4 copy.51
  10.5 1.4 convert_reduce_fusion
  12.7 9.5 all_gather.57
  22.3 8.3 all_gather.55
  31.2 26.0 %all-gather.15.cloned.1.call-done = bf16[1024,3,512]{0,2,1:T(8,128)(2,1)} async-done(((bf16[256,3,512]{0,2,1:T(8,128)(2,1)}), bf16[1024,3,512]{0,2,1:T(8,128)(2,1)}) %all-gather.15.cloned.1.call-update) | async-done | bytes 3145744 | tf_op jit(solution)/shard_map/all_gather | solution.py:97
  57.2 3.9 convolution_add_fusion
  64.1 2.1 slice.168
  67.5 11.9 all-gather
  80.6 4.9 all-gather.21.cloned.1.call-done
  85.5 2.8 fusion.75
  89.5 44.2 %all-gather.19.cloned.1.call-done = bf16[2048,8,64]{0,2,1:T(8,128)(2,1)} async-done(((bf16[512,8,64]{0,2,1:T(8,128)(2,1)}), bf16[2048,8,64]{0,2,1:T(8,128)(2,1)}) %all-gather.19.cloned.1.call-update) | async-done | bytes 2097168 | tf_op jit(solution)/shard_map/all_gather | solution.py:127
  133.6 16.0 %fusion = (f32[8,512]{1,0:T(8,128)S(1)}, f32[8,512,2048]{2,1,0:T(8,128)}) fusion(pred[512,2048]{1,0:T(8,128)(4,1)S(1)} %fusion.7, bf16[2048,8,64]{0,2,1:T(8,128)(2,1)} %all-gather.19.cloned.1.call-done, bf16[512,8,48]{0,2,1:T(8,128)(2,1)S(1)} %slice.170, bf16[512,8,8]{0,2,1:T(8,128)(2,1)} %get-tuple-element.148, bf16[512,8,8]{0,2,1:T(8,128)(2,1)} %get-tuple-element.147), kind=kOutput, calls=%fused_computation.4 | convolution fusion | flops 1100476416 | bytes 37240832 | tf_op jit(solution)/shard_map/while/body/eval_jaxpr/qhe,khe->hqk/dot_general | solution.py:55
  149.6 15.9 %exponential_reduce_fusion = f32[8,512]{1,0:T(8,128)S(1)} fusion(f32[8,512,2048]{2,1,0:T(8,128)} %get-tuple-element.176, f32[8,512]{1,0:T(8,128)S(1)} %get-tuple-element.175, pred[512,2048]{1,0:T(8,128)(4,1)S(1)} %fusion.7), kind=kLoop, calls=%fused_computation.2 | loop fusion | flops 33550336 | bytes 34635776 | tf_op jit(solution)/shard_map/while/body/eval_jaxpr/reduce_sum | solution.py:144
  165.5 4.6 copy-done
  170.1 9.4 exponential_convert_fusion
  180.3 12.4 multiply_reduce_fusion.2
  192.7 25.3 %multiply_convert_fusion = bf16[8,512,2048]{2,1,0:T(8,128)(2,1)} fusion(bf16[8,512,2048]{2,1,0:T(8,128)(2,1)} %exponential_convert_fusion, bf16[512,8,64]{0,2,1:T(8,128)(2,1)S(1)} %bitcast.212, bf16[2048,8,64]{0,2,1:T(8,128)(2,1)} %all-gather.17.cloned.1.call-done, f32[8,512]{1,0:T(8,128)S(1)} %bitcast.227), kind=kOutput, calls=%fused_computation | convolution fusion | flops 1107296256 | bytes 36192256 | tf_op jit(solution)/shard_map/while/body/eval_jaxpr/qhe,khe->hqk/dot_general | solution.py:189
  218.1 10.9 convolution_multiply_fusion
  228.9 5.4 copy.52
  234.3 10.9 fusion.82
  245.2 5.4 copy.53
  250.6 8.2 pad_maximum_fusion
  259.4 8.0 all-gather.1
  267.5 15.1 %multiply_convert_fusion.1 = (bf16[512,2048]{1,0:T(8,128)(2,1)}, f32[512,2048]{1,0:T(8,128)}, f32[512,2048]{1,0:T(8,128)}) fusion(f32[2048]{0:T(1024)S(1)} %bitcast.253, bf16[1024,2048]{1,0:T(8,128)(2,1)} %all-gather.23.cloned.1.call-done, bf16[1,512,1024]{2,1,0:T(8,128)(2,1)S(1)} %copy-done.3, f32[1024]{0:T(1024)S(1)} %bitcast.257, f32[1024]{0:T(1024)S(1)} %bitcast.234, ...), kind=kOutput, calls=%fused_computation.9 | convolution fusion | flops 2219835392 | bytes 15749120 | tf_op jit(solution)/shard_map/dot_general | solution.py:152
  282.6 5.2 all-gather.25.cloned.1.call-done
  287.8 7.4 fusion.72
  295.2 1.3 copy-done.32
  296.6 5.8 fusion.46
  302.5 7.2 fusion.73
  310.2 6.7 fusion.81
  316.9 3.7 fusion.48
  320.6 12.7 fusion.41
  333.2 2.1 slice.136
  335.3 4.2 convolution_add_fusion.1
  339.6 95.1 %reduce-scatter.12.cloned.1.call-done = f32[512,1024]{1,0:T(8,128)} async-done(((f32[2048,1024]{1,0:T(8,128)}), f32[512,1024]{1,0:T(8,128)}) %reduce-scatter.12.cloned.1.call-update) | async-done | bytes 2097168 | tf_op jit(solution)/shard_map/reduce_scatter | solution.py:214
  434.6 3.0 fusion.68
  437.7 2.5 copy.54
  442.6 2.8 pad_maximum_fusion.2
  445.4 2.6 copy.55
  448.0 2.5 copy.56
  450.5 6.0 convolution_bitcast_fusion
  457.2 6.6 fusion.55
  463.9 3.1 fusion.43
  467.1 2.1 fusion.20
  470.1 149.9 %reduce-scatter.18.cloned.1.call-done = f32[64,2048]{1,0:T(8,128)} async-done(((f32[1024,2048]{1,0:T(8,128)}), f32[64,2048]{1,0:T(8,128)}) %reduce-scatter.18.cloned.1.call-update) | async-done | bytes 524304 | tf_op jit(solution)/shard_map/reduce_scatter | solution.py:258
  620.1 182.1 %reduce-scatter.20.cloned.1.call-done = f32[2048,64]{0,1:T(8,128)} async-done(((f32[2048,1024]{0,1:T(8,128)}), f32[2048,64]{0,1:T(8,128)}) %reduce-scatter.20.cloned.1.call-update) | async-done | bytes 524304 | tf_op jit(solution)/shard_map/reduce_scatter | solution.py:259
  802.4 33.3 %all-reduce.4.cloned.1.call-done = (f32[512,1024]{1,0:T(8,128)}, f32[512,1024]{1,0:T(8,128)}, f32[512,1024]{1,0:T(8,128)}) async-done(((f32[512,1024]{1,0:T(8,128)}, f32[512,1024]{1,0:T(8,128)}, f32[512,1024]{1,0:T(8,128)}), (f32[512,1024]{1,0:T(8,128)}, f32[512,1024]{1,0:T(8,128)}, f32[512,1024]{1,0:T(8,128)})) %all-reduce.4.cloned.1.call-update) | async-done | bytes 6291472 | tf_op jit(solution)/shard_map/psum | solution.py:157
  835.7 3.4 fusion.35
  840.2 137.3 %reduce-scatter.14.cloned.1.call-done = f32[64,3,512]{2,0,1:T(8,128)} async-done(((f32[1024,3,512]{2,0,1:T(8,128)}), f32[64,3,512]{2,0,1:T(8,128)}) %reduce-scatter.14.cloned.1.call-update) | async-done | bytes 393232 | tf_op jit(solution)/shard_map/reduce_scatter | solution.py:256
  978.8 39.4 %all-reduce = f32[2048]{0:T(1024)S(1)} all-reduce(f32[2048]{0:T(1024)S(1)} %get-tuple-element.179), channel_id=9, replica_groups=mesh['fsdp'=4,'ctx'=4,'tp'=2] {'fsdp','ctx'}, use_global_device_ids=true, to_apply=%region_25.26.clone | all-reduce | flops 2048 | bytes 16384
  1018.3 7.8 all-gather.4
  1026.1 36.4 %reduce-scatter.16.cloned.1.call-done = f32[512,64]{0,1:T(8,128)} async-done(((f32[512,1024]{0,1:T(8,128)}), f32[512,64]{0,1:T(8,128)}) %reduce-scatter.16.cloned.1.call-update) | async-done | bytes 131088 | tf_op jit(solution)/shard_map/reduce_scatter | solution.py:257
  1062.5 15.7 %all_gather.68 = f32[512,256]{0,1:T(8,128)} all-gather(f32[512,64]{0,1:T(8,128)} %reduce-scatter.16.cloned.1.call-done), channel_id=1, replica_groups=mesh['fsdp'=4,'ctx'=4,'tp'=2] {'ctx'}, dimensions={1}, use_global_device_ids=true | all-gather | bytes 655360 | tf_op jit(solution)/shard_map/all_gather | solution.py:266
  1078.2 2.0 copy.61
  1080.2 57.7 %reduce-scatter.24.cloned.1.call-done = f32[32,3]{1,0:T(8,128)} async-done(((f32[512,3]{1,0:T(8,128)}), f32[32,3]{1,0:T(8,128)}) %reduce-scatter.24.cloned.1.call-update) | async-done | bytes 400
  1138.7 12.2 all-gather.3
  1151.6 30.2 %all-gather.29.cloned.1.call-done = f32[256,2048]{1,0:T(8,128)} async-done(((f32[64,2048]{1,0:T(8,128)}), f32[256,2048]{1,0:T(8,128)}) %all-gather.29.cloned.1.call-update) | async-done | bytes 2097168 | tf_op jit(solution)/shard_map/all_gather | solution.py:267
  1181.7 46.1 %all-gather.31.cloned.1.call-done = f32[2048,256]{0,1:T(8,128)} async-done(((f32[2048,64]{0,1:T(8,128)}), f32[2048,256]{0,1:T(8,128)}) %all-gather.31.cloned.1.call-update) | async-done | bytes 2097168 | tf_op jit(solution)/shard_map/all_gather | solution.py:268
  1227.8 2.9 copy.62
  1230.7 4.9 fusion.31
  1235.6 70.6 %reduce-scatter.22.cloned.1.call-done = f32[64,6]{1,0:T(8,128)} async-done(((f32[1024,6]{1,0:T(8,128)}), f32[64,6]{1,0:T(8,128)}) %reduce-scatter.22.cloned.1.call-update) | async-done | bytes 1552
  1307.1 13.4 all-gather.2
  1321.1 20.2 %all-gather.27.cloned.1.call-done = f32[256,3,512]{2,0,1:T(8,128)} async-done(((f32[64,3,512]{2,0,1:T(8,128)}), f32[256,3,512]{2,0,1:T(8,128)}) %all-gather.27.cloned.1.call-update) | async-done | bytes 1572880 | tf_op jit(solution)/shard_map/all_gather | solution.py:265
  1341.3 2.7 copy.76
  (150 shorter events, 21.8 us)
Async XLA Ops:
  7.2 4.8 copy-start.2
  7.2 5.2 copy-start.21
  7.2 5.4 copy-start.25
  7.2 5.4 copy-start.26
  7.2 5.4 copy-start.27
  7.2 5.4 copy-start.28
  7.2 5.4 copy-start.29
  7.3 5.4 copy-start.30
  7.3 5.4 copy-start.22
  7.3 49.9 %all-gather.15.cloned.1.call-start = ((), (), s32[]{:S(2)}) async-start(), calls=%async_computation.7 | async-start | bytes 3932160 | tf_op jit(solution)/shard_map/all_gather | solution.py:97
  9.7 75.8 %all-gather.21.cloned.1.call-start = ((), (), s32[]{:S(2)}) async-start(), calls=%async_computation.10 | async-start | bytes 1310720 | tf_op jit(solution)/shard_map/all_gather | solution.py:98
  10.5 123.2 %all-gather.19.cloned.1.call-start = ((), (), s32[]{:S(2)}) async-start(), calls=%async_computation.9 | async-start | bytes 2621440 | tf_op jit(solution)/shard_map/all_gather | solution.py:127
  12.5 48.8 %copy-start.10 = (f32[512,8]{0,1:T(8,128)}, f32[512,8]{0,1:T(8,128)S(1)}, u32[]{:S(2)}) copy-start(f32[512,8]{0,1:T(8,128)S(1)} %get-tuple-element.171) | copy-start | bytes 49156
  12.6 48.8 %copy-start.12 = (f32[512,8]{0,1:T(8,128)}, f32[512,8]{0,1:T(8,128)S(1)}, u32[]{:S(2)}) copy-start(f32[512,8]{0,1:T(8,128)S(1)} %get-tuple-element.172) | copy-start | bytes 49156
  31.2 29.9 %copy-start.14 = (f32[1,1024]{1,0:T(1,128)}, f32[1,1024]{1,0:T(1,128)S(1)}, u32[]{:S(2)}) copy-start(f32[1,1024]{1,0:T(1,128)S(1)} %get-tuple-element.161) | copy-start | bytes 12292
  31.2 29.9 %copy-start.18 = (f32[1,1024]{1,0:T(1,128)}, f32[1,1024]{1,0:T(1,128)S(1)}, u32[]{:S(2)}) copy-start(f32[1,1024]{1,0:T(1,128)S(1)} %get-tuple-element.162) | copy-start | bytes 12292
  61.1 2.1 copy-start.6
  61.3 1.1 copy-start.5
  61.3 6.1 copy-start.20
  61.3 24.2 %copy-start.1 = (f32[1,512,1024]{2,1,0:T(8,128)S(1)}, f32[1,512,1024]{2,1,0:T(8,128)}, u32[]{:S(2)}) copy-start(f32[1,512,1024]{2,1,0:T(8,128)} %param.31) | copy-start | bytes 6291460
  64.1 116.3 %all-gather.17.cloned.1.call-start = ((), (), s32[]{:S(2)}) async-start(), calls=%async_computation.8 | async-start | bytes 2621440 | tf_op jit(solution)/shard_map/all_gather | solution.py:128
  66.2 201.3 %all-gather.23.cloned.1.call-start = ((), (), s32[]{:S(2)}) async-start(), calls=%async_computation.11 | async-start | bytes 5242880 | tf_op jit(solution)/shard_map/all_gather | solution.py:99
  66.8 221.0 %all-gather.25.cloned.1.call-start = ((), (), s32[]{:S(2)}) async-start(), calls=%async_computation.12 | async-start | bytes 5242880 | tf_op jit(solution)/shard_map/all_gather | solution.py:100
  67.4 367.3 %reduce-scatter.12.cloned.1.call-start = ((), (), s32[]{:S(2)}) async-start(), calls=%async_computation.13 | async-start | bytes 10485760 | tf_op jit(solution)/shard_map/reduce_scatter | solution.py:214
  149.6 20.5 %copy-start = (f32[8,512,2048]{2,1,0:T(8,128)S(1)}, f32[8,512,2048]{2,1,0:T(8,128)}, u32[]{:S(2)}) copy-start(f32[8,512,2048]{2,1,0:T(8,128)} %get-tuple-element.176) | copy-start | bytes 100663296
  179.5 13.3 copy-start.4
  192.7 25.3 %copy-start.8 = (bf16[512,8,8]{0,2,1:T(8,128)(2,1)S(1)}, bf16[512,8,8]{0,2,1:T(8,128)(2,1)}, u32[]{:S(2)}) copy-start(bf16[512,8,8]{0,2,1:T(8,128)(2,1)} %get-tuple-element.147) | copy-start | bytes 196612
  192.7 25.3 %copy-start.9 = (bf16[512,8,8]{0,2,1:T(8,128)(2,1)S(1)}, bf16[512,8,8]{0,2,1:T(8,128)(2,1)}, u32[]{:S(2)}) copy-start(bf16[512,8,8]{0,2,1:T(8,128)(2,1)} %get-tuple-element.148) | copy-start | bytes 196612
  258.7 0.7 copy-start.23
  258.7 8.8 copy-start.3
  258.8 361.2 %reduce-scatter.18.cloned.1.call-start = ((), (), s32[]{:S(2)}) async-start(), calls=%async_computation.17 | async-start | bytes 8912896 | tf_op jit(solution)/shard_map/reduce_scatter | solution.py:258
  295.2 1.3 copy-start.32
  302.4 499.7 %reduce-scatter.20.cloned.1.call-start = ((), (), s32[]{:S(2)}) async-start(), calls=%async_computation.19 | async-start | bytes 8912896 | tf_op jit(solution)/shard_map/reduce_scatter | solution.py:259
  309.7 526.0 %all-reduce.4.cloned.1.call-start = ((), (), s32[]{:S(2)}) async-start(), calls=%async_computation.23 | async-start | bytes 12582912 | tf_op jit(solution)/shard_map/psum | solution.py:157
  310.2 6.7 copy-start.24
  310.2 6.7 copy-start.33
  339.6 101.9 %copy-start.11 = (f32[512,8]{0,1:T(8,128)S(1)}, f32[512,8]{0,1:T(8,128)}, u32[]{:S(2)}) copy-start(f32[512,8]{0,1:T(8,128)} %copy-done.10) | copy-start | bytes 49156
  339.6 101.9 %copy-start.13 = (f32[512,8]{0,1:T(8,128)S(1)}, f32[512,8]{0,1:T(8,128)}, u32[]{:S(2)}) copy-start(f32[512,8]{0,1:T(8,128)} %copy-done.12) | copy-start | bytes 49156
  456.5 0.7 copy-start.15
  456.5 0.7 copy-start.19
  456.6 520.9 %reduce-scatter.14.cloned.1.call-start = ((), (), s32[]{:S(2)}) async-start(), calls=%async_computation.14 | async-start | bytes 6684672 | tf_op jit(solution)/shard_map/reduce_scatter | solution.py:256
  463.8 598.7 %reduce-scatter.16.cloned.1.call-start = ((), (), s32[]{:S(2)}) async-start(), calls=%async_computation.16 | async-start | bytes 2228224 | tf_op jit(solution)/shard_map/reduce_scatter | solution.py:257
  467.0 670.9 %reduce-scatter.24.cloned.1.call-start = ((), (), s32[]{:S(2)}) async-start(), calls=%async_computation.22 | async-start | bytes 278528
  470.0 711.7 %all-gather.29.cloned.1.call-start = ((), (), s32[]{:S(2)}) async-start(), calls=%async_computation.18 | async-start | bytes 2621440 | tf_op jit(solution)/shard_map/all_gather | solution.py:267
  620.0 607.8 %all-gather.31.cloned.1.call-start = ((), (), s32[]{:S(2)}) async-start(), calls=%async_computation.20 | async-start | bytes 2621440 | tf_op jit(solution)/shard_map/all_gather | solution.py:268
  802.2 175.4 %copy-start.31 = (u32[32]{0:T(128)S(1)}, u32[32]{0:T(128)}, u32[]{:S(2)}) copy-start(u32[32]{0:T(128)} %constant.141) | copy-start | bytes 388
  802.2 504.0 %reduce-scatter.22.cloned.1.call-start = ((), (), s32[]{:S(2)}) async-start(), calls=%async_computation.21 | async-start | bytes 557056
  839.1 391.6 %copy-start.16 = (f32[1,1024]{1,0:T(1,128)S(1)}, f32[1,1024]{1,0:T(1,128)}, u32[]{:S(2)}) copy-start(f32[1,1024]{1,0:T(1,128)} %get-tuple-element.159) | copy-start | bytes 12292
  839.1 391.6 %copy-start.17 = (f32[1,1024]{1,0:T(1,128)S(1)}, f32[1,1024]{1,0:T(1,128)}, u32[]{:S(2)}) copy-start(f32[1,1024]{1,0:T(1,128)} %get-tuple-element.160) | copy-start | bytes 12292
  840.2 501.1 %all-gather.27.cloned.1.call-start = ((), (), s32[]{:S(2)}) async-start(), calls=%async_computation.15 | async-start | bytes 1966080 | tf_op jit(solution)/shard_map/all_gather | solution.py:265
  1235.6 108.4 %copy-start.7 = (f32[256,2048]{1,0:T(8,128)S(1)}, f32[256,2048]{1,0:T(8,128)}, u32[]{:S(2)}) copy-start(f32[256,2048]{1,0:T(8,128)} %all-gather.29.cloned.1.call-done) | copy-start | bytes 6291460
Sparse Core Ops, SparseCore 0:
  10.5 46.6 all-gather.14
  59.0 26.4 all-gather.20
  87.7 45.9 all-gather.18
  135.6 44.6 all-gather.16
  182.0 51.4 all-gather.22
  235.2 52.6 all-gather.24
  290.2 144.4 reduce-scatter.11
  436.9 183.0 reduce-scatter.17
  622.3 179.8 reduce-scatter.19
  805.9 29.7 all-reduce.3
  838.1 139.3 reduce-scatter.13
  980.3 82.1 reduce-scatter.15
  1064.8 73.0 reduce-scatter.23
  1139.3 42.3 all-gather.28
  1183.1 44.6 all-gather.30
  1230.5 75.7 reduce-scatter.21
  1307.7 33.5 all-gather.26
where the time goes:
time: 1360 us; the launch traced here: 1350 us
  waiting for transfers between devices  942 us (69%)
  matrix products  161 us (12%)
  blocking collectives  126 us (9%)
  local copies, waits for them, and re-layouts  54.5 us (4%)
  other arithmetic  52.6 us (4%)
  between operations  15.4 us (1%)
    reduce_scatter x1, waiting for transfers between devices, local(): lax.psum_scatter(grad_down_w, ('fsdp', 'ctx'), scatter_dimension=1, tiled...  182 us
    reduce_scatter x1, waiting for transfers between devices, local(): lax.psum_scatter(grad_up_w, ('fsdp', 'ctx'), scatter_dimension=0, tiled=T...  150 us
    reduce_scatter x1, waiting for transfers between devices, local(): lax.psum_scatter(grad_joint_w, ('fsdp', 'ctx'), scatter_dimension=0, tile...  137 us
    unnamed x19, waiting for transfers between devices  130 us
    reduce_scatter x1, waiting for transfers between devices, local(): lax.psum_scatter(jnp.concatenate([key_part.reshape(count_rows * lax.axis_...  95.1 us
    all_gather x1, waiting for transfers between devices, local(): lax.all_gather(share_down, 'ctx', axis=1, tiled=True)  46.1 us
    all_gather x1, waiting for transfers between devices, local(): lax.all_gather(keys_here, 'ctx', axis=0, tiled=True)  44.2 us
    unnamed x1, blocking collectives  39.4 us
  transfers between devices with their start and end apart: 17, of which 16 were waited for; matrix products, arithmetic and copies ran while one was open for 19% of the time, Pallas kernels for 0%

commit v1 on v0

--- a/solution.py
+++ b/solution.py
@@ -261,10 +261,28 @@
         lax.psum_scatter(grad_joint_b, ("fsdp", "ctx"), scatter_dimension=1, tiled=True),
         lax.psum_scatter(grad_up_b, ("fsdp", "ctx"), scatter_dimension=0, tiled=True),
     )
+
+    def body_replace(link_axis, vector):
+        total_devices = lax.axis_size(link_axis)
+        log = tuple(((i0, (i0 + 1) % total_devices) for i0 in range(total_devices)))
+        rack = tuple(((i0, (i0 - 1) % total_devices) for i0 in range(total_devices)))
+        step_out, b_now = ([vector], [vector])
+        for _ in range(total_devices // 2):
+            block_now = lax.ppermute(step_out[-1], link_axis, log)
+            step_out.append(block_now)
+        q = 0
+        while q < (total_devices - 1) // 2:
+            seen_now = lax.ppermute(b_now[-1], link_axis, rack)
+            b_now.append(seen_now)
+            q = q + 1
+        finding = jnp.concatenate([*step_out[::-1], *b_now[1:]], axis=0)
+        now = lax.axis_index(link_axis)
+        return jnp.roll(finding, (now - total_devices // 2) * vector.shape[0], 0)
+
     owned = (
         lax.all_gather(share_joint, "ctx", axis=0, tiled=True),
         lax.all_gather(share_output, "ctx", axis=1, tiled=True),
-        lax.all_gather(share_up, "ctx", axis=0, tiled=True),
+        body_replace("ctx", share_up),
         lax.all_gather(share_down, "ctx", axis=1, tiled=True),
         lax.all_gather(share_small, "ctx", axis=1, tiled=True),
         lax.all_gather(share_jbias, "ctx", axis=1, tiled=True),

time: 1360 us -> 1320 us (0.971)
  waiting for transfers between devices: 942 us -> 863 us
  local copies, waits for them, and re-layouts: 54.5 us -> 72.7 us
  blocking collectives: 126 us -> 143 us
    reduce_scatter x1, waiting for transfers between devices: 36.4 us -> 1.88 us  [local(): lax.psum_scatter(grad_output_w, ('fsdp', 'ctx'), scatter_dimension=1, til...]
    reduce_scatter x1, waiting for transfers between devices: 150 us -> 182 us  [local(): lax.psum_scatter(grad_up_w, ('fsdp', 'ctx'), scatter_dimension=0, tiled=T...]
    psum x1, waiting for transfers between devices: 33.3 us -> 2.5 us  [local(): mixed_all = lax.psum(partial_value, 'tp')]
    all_gather x1 -> x0, waiting for transfers between devices: 30.2 us -> none  [local(): lax.all_gather(share_up, 'ctx', axis=0, tiled=True)]
    reduce_scatter x1, waiting for transfers between devices: 182 us -> 153 us  [local(): lax.psum_scatter(grad_down_w, ('fsdp', 'ctx'), scatter_dimension=1, tiled...]
    ppermute x0 -> x3, waiting for transfers between devices: none -> 24 us  [the longest x2 22.4 us: body_replace(): block_now = lax.ppermute(step_out[-1], link_axis, log)]
    unnamed x1, blocking collectives: 39.4 us -> 55.4 us
    all_gather x1, waiting for transfers between devices: 46.1 us -> 30.3 us  [local(): lax.all_gather(share_down, 'ctx', axis=1, tiled=True)]
  transfers between devices with their start and end apart: 17 -> 19, of which waited for: 16 -> 16; matrix products, arithmetic and copies ran while one was open for 19% -> 21% of each run, Pallas kernels for 0% -> 0%
where the time goes in v1:
time: 1320 us; the launch traced here: 1310 us
  waiting for transfers between devices  863 us (65%)
  matrix products  159 us (12%)
  blocking collectives  143 us (11%)
  local copies, waits for them, and re-layouts  72.7 us (6%)
  other arithmetic  53.3 us (4%)
  between operations  15.4 us (1%)
    reduce_scatter x1, waiting for transfers between devices, local(): lax.psum_scatter(grad_up_w, ('fsdp', 'ctx'), scatter_dimension=0, tiled=T...  182 us
    reduce_scatter x1, waiting for transfers between devices, local(): lax.psum_scatter(grad_down_w, ('fsdp', 'ctx'), scatter_dimension=1, tiled...  153 us
    unnamed x18, waiting for transfers between devices  141 us
    reduce_scatter x1, waiting for transfers between devices, local(): lax.psum_scatter(grad_joint_w, ('fsdp', 'ctx'), scatter_dimension=0, tile...  135 us
    reduce_scatter x1, waiting for transfers between devices, local(): lax.psum_scatter(jnp.concatenate([key_part.reshape(count_rows * lax.axis_...  97.6 us
    unnamed x1, blocking collectives  55.4 us
    all_gather x1, waiting for transfers between devices, local(): lax.all_gather(keys_here, 'ctx', axis=0, tiled=True)  44.2 us
    unnamed x89, local copies, waits for them, and re-layouts  38.1 us
  transfers between devices with their start and end apart: 19, of which 16 were waited for; matrix products, arithmetic and copies ran while one was open for 21% of the time, Pallas kernels for 0%

profile of v1, /device:TPU:0, one launch (start us, length us, event | category | flops | bytes accessed | tf_op | source)
XLA Modules:
  0.0 1310.1 jit_solution(4276016261239933987)
XLA Ops:
  7.3 2.4 copy.51
  13.4 9.5 all_gather.54
  22.9 8.3 all_gather.52
  31.9 25.3 %all-gather.14.cloned.1.call-done = bf16[1024,3,512]{0,2,1:T(8,128)(2,1)} async-done(((bf16[256,3,512]{0,2,1:T(8,128)(2,1)}), bf16[1024,3,512]{0,2,1:T(8,128)(2,1)}) %all-gather.14.cloned.1.call-update) | async-done | bytes 3145744 | tf_op jit(solution)/shard_map/all_gather | solution.py:97
  57.2 3.9 convolution_add_fusion
  64.1 2.1 slice.168
  67.5 11.9 all-gather
  80.6 4.9 all-gather.20.cloned.1.call-done
  85.5 2.8 fusion.75
  89.5 44.2 %all-gather.18.cloned.1.call-done = bf16[2048,8,64]{0,2,1:T(8,128)(2,1)} async-done(((bf16[512,8,64]{0,2,1:T(8,128)(2,1)}), bf16[2048,8,64]{0,2,1:T(8,128)(2,1)}) %all-gather.18.cloned.1.call-update) | async-done | bytes 2097168 | tf_op jit(solution)/shard_map/all_gather | solution.py:127
  133.6 16.0 %fusion = (f32[8,512]{1,0:T(8,128)S(1)}, f32[8,512,2048]{2,1,0:T(8,128)}) fusion(pred[512,2048]{1,0:T(8,128)(4,1)S(1)} %fusion.7, bf16[2048,8,64]{0,2,1:T(8,128)(2,1)} %all-gather.18.cloned.1.call-done, bf16[512,8,48]{0,2,1:T(8,128)(2,1)S(1)} %slice.170, bf16[512,8,8]{0,2,1:T(8,128)(2,1)} %get-tuple-element.148, bf16[512,8,8]{0,2,1:T(8,128)(2,1)} %get-tuple-element.147), kind=kOutput, calls=%fused_computation.4 | convolution fusion | flops 1100476416 | bytes 37240832 | tf_op jit(solution)/shard_map/while/body/eval_jaxpr/qhe,khe->hqk/dot_general | solution.py:55
  149.6 15.9 %exponential_reduce_fusion = f32[8,512]{1,0:T(8,128)S(1)} fusion(f32[8,512,2048]{2,1,0:T(8,128)} %get-tuple-element.176, f32[8,512]{1,0:T(8,128)S(1)} %get-tuple-element.175, pred[512,2048]{1,0:T(8,128)(4,1)S(1)} %fusion.7), kind=kLoop, calls=%fused_computation.2 | loop fusion | flops 33550336 | bytes 34635776 | tf_op jit(solution)/shard_map/while/body/eval_jaxpr/reduce_sum | solution.py:144
  165.5 4.6 copy-done
  170.1 9.4 exponential_convert_fusion
  180.3 12.4 multiply_reduce_fusion.2
  192.7 25.7 %multiply_convert_fusion = bf16[8,512,2048]{2,1,0:T(8,128)(2,1)} fusion(bf16[8,512,2048]{2,1,0:T(8,128)(2,1)} %exponential_convert_fusion, bf16[512,8,64]{0,2,1:T(8,128)(2,1)S(1)} %bitcast.212, bf16[2048,8,64]{0,2,1:T(8,128)(2,1)} %all-gather.16.cloned.1.call-done, f32[8,512]{1,0:T(8,128)S(1)} %bitcast.227), kind=kOutput, calls=%fused_computation | convolution fusion | flops 1107296256 | bytes 36192256 | tf_op jit(solution)/shard_map/while/body/eval_jaxpr/qhe,khe->hqk/dot_general | solution.py:189
  218.5 10.9 convolution_multiply_fusion
  229.4 5.4 copy.52
  234.7 10.9 fusion.82
  245.6 5.4 copy.53
  251.0 8.2 pad_maximum_fusion
  259.8 8.1 all-gather.1
  267.9 14.7 %multiply_convert_fusion.1 = (bf16[512,2048]{1,0:T(8,128)(2,1)S(1)}, f32[512,2048]{1,0:T(8,128)}, f32[512,2048]{1,0:T(8,128)}) fusion(f32[2048]{0:T(1024)S(1)} %bitcast.253, bf16[1024,2048]{1,0:T(8,128)(2,1)} %all-gather.22.cloned.1.call-done, bf16[1,512,1024]{2,1,0:T(8,128)(2,1)S(1)} %copy-done.3, f32[1024]{0:T(1024)S(1)} %bitcast.257, ...), kind=kOutput, calls=%fused_computation.9 | convolution fusion | flops 2219835392 | bytes 15749120 | tf_op jit(solution)/shard_map/dot_general | solution.py:152
  283.9 5.7 fusion.73
  289.7 7.5 fusion.72
  298.5 5.8 fusion.46
  304.3 3.1 fusion.43
  308.0 6.6 fusion.81
  314.6 3.7 fusion.48
  318.3 12.6 fusion.41
  330.8 2.1 slice.136
  332.9 4.1 convolution_add_fusion.1
  337.1 97.6 %reduce-scatter.12.cloned.1.call-done = f32[512,1024]{1,0:T(8,128)} async-done(((f32[2048,1024]{1,0:T(8,128)}), f32[512,1024]{1,0:T(8,128)}) %reduce-scatter.12.cloned.1.call-update) | async-done | bytes 2097168 | tf_op jit(solution)/shard_map/reduce_scatter | solution.py:214
  434.6 3.0 fusion.68
  437.7 2.6 copy.54
  442.6 2.8 pad_maximum_fusion.2
  445.4 2.6 copy.55
  448.0 2.5 copy.56
  450.6 6.0 convolution_bitcast_fusion
  457.3 6.6 fusion.55
  463.9 2.1 fusion.20
  467.0 153.0 %reduce-scatter.20.cloned.1.call-done = f32[2048,64]{0,1:T(8,128)} async-done(((f32[2048,1024]{0,1:T(8,128)}), f32[2048,64]{0,1:T(8,128)}) %reduce-scatter.20.cloned.1.call-update) | async-done | bytes 524304 | tf_op jit(solution)/shard_map/reduce_scatter | solution.py:259
  620.1 182.1 %reduce-scatter.18.cloned.1.call-done = f32[64,2048]{1,0:T(8,128)} async-done(((f32[1024,2048]{1,0:T(8,128)}), f32[64,2048]{1,0:T(8,128)}) %reduce-scatter.18.cloned.1.call-update) | async-done | bytes 524304 | tf_op jit(solution)/shard_map/reduce_scatter | solution.py:258
  802.1 22.4 %collective-permute-done = f32[64,2048]{1,0:T(8,128)} collective-permute-done((f32[64,2048]{1,0:T(8,128)}, f32[64,2048]{1,0:T(8,128)}, u32[]{:S(2)}, u32[]{:S(2)}) %collective-permute-start) | collective-permute-done | bytes 524320 | tf_op jit(solution)/shard_map/ppermute | solution.py:271
  825.9 55.4 %all-reduce = f32[2048]{0:T(1024)S(1)} all-reduce(f32[2048]{0:T(1024)S(1)} %get-tuple-element.179), channel_id=9, replica_groups=mesh['fsdp'=4,'ctx'=4,'tp'=2] {'fsdp','ctx'}, use_global_device_ids=true, to_apply=%region_25.26.clone | all-reduce | flops 2048 | bytes 16384
  881.4 7.5 all-gather.4
  890.8 17.1 %all_gather.65 = f32[512,256]{0,1:T(8,128)} all-gather(f32[512,64]{0,1:T(8,128)} %reduce-scatter.16.cloned.1.call-done), channel_id=1, replica_groups=mesh['fsdp'=4,'ctx'=4,'tp'=2] {'ctx'}, dimensions={1}, use_global_device_ids=true | all-gather | bytes 655360 | tf_op jit(solution)/shard_map/all_gather | solution.py:284
  907.8 2.0 copy.61
  909.9 2.0 collective-permute-start.2
  915.7 1.9 constant_dynamic-update-slice_fusion.5
  920.9 2.0 constant_dynamic-update-slice_fusion.3
  923.0 2.5 all-reduce.4.cloned.1.call-done
  925.5 3.4 fusion.35
  931.9 135.2 %reduce-scatter.14.cloned.1.call-done = f32[64,3,512]{2,0,1:T(8,128)} async-done(((f32[1024,3,512]{2,0,1:T(8,128)}), f32[64,3,512]{2,0,1:T(8,128)}) %reduce-scatter.14.cloned.1.call-update) | async-done | bytes 393232 | tf_op jit(solution)/shard_map/reduce_scatter | solution.py:256
  1070.9 3.1 constant_dynamic-slice_fusion
  1074.1 68.8 %reduce-scatter.24.cloned.1.call-done = f32[32,3]{1,0:T(8,128)} async-done(((f32[512,3]{1,0:T(8,128)}), f32[32,3]{1,0:T(8,128)}) %reduce-scatter.24.cloned.1.call-update) | async-done | bytes 400
  1143.6 12.1 all-gather.3
  1156.4 30.3 %all-gather.28.cloned.1.call-done = f32[2048,256]{0,1:T(8,128)} async-done(((f32[2048,64]{0,1:T(8,128)}), f32[2048,256]{0,1:T(8,128)}) %all-gather.28.cloned.1.call-update) | async-done | bytes 2097168 | tf_op jit(solution)/shard_map/all_gather | solution.py:286
  1186.7 2.9 copy.62
  1189.6 4.8 fusion.31
  1194.5 70.6 %reduce-scatter.22.cloned.1.call-done = f32[64,6]{1,0:T(8,128)} async-done(((f32[1024,6]{1,0:T(8,128)}), f32[64,6]{1,0:T(8,128)}) %reduce-scatter.22.cloned.1.call-update) | async-done | bytes 1552
  1265.9 13.4 %all-gather.2 = f32[4,64,6]{1,2,0:T(8,128)S(1)} all-gather(f32[1,64,6]{1,2,0:T(8,128)S(1)} %bitcast.243), channel_id=1, replica_groups=mesh['fsdp'=4,'ctx'=4,'tp'=2] {'ctx'}, dimensions={0}, use_global_device_ids=true | all-gather | bytes 7680 | tf_op jit(solution)/shard_map/all_gather | solution.py:287
  1279.9 20.2 %all-gather.26.cloned.1.call-done = f32[256,3,512]{2,0,1:T(8,128)} async-done(((f32[64,3,512]{2,0,1:T(8,128)}), f32[256,3,512]{2,0,1:T(8,128)}) %all-gather.26.cloned.1.call-update) | async-done | bytes 1572880 | tf_op jit(solution)/shard_map/all_gather | solution.py:283
  1300.1 2.7 copy.82
  (161 shorter events, 39.9 us)
Async XLA Ops:
  7.2 5.4 copy-start.2
  7.2 6.0 copy-start.25
  7.2 6.1 copy-start.26
  7.2 6.1 copy-start.27
  7.2 6.1 copy-start.28
  7.2 6.1 copy-start.29
  7.2 6.1 copy-start.30
  7.3 6.1 copy-start.22
  7.3 49.9 %all-gather.14.cloned.1.call-start = ((), (), s32[]{:S(2)}) async-start(), calls=%async_computation.7 | async-start | bytes 3932160 | tf_op jit(solution)/shard_map/all_gather | solution.py:97
  9.7 75.8 %all-gather.20.cloned.1.call-start = ((), (), s32[]{:S(2)}) async-start(), calls=%async_computation.10 | async-start | bytes 1310720 | tf_op jit(solution)/shard_map/all_gather | solution.py:98
  10.4 123.2 %all-gather.18.cloned.1.call-start = ((), (), s32[]{:S(2)}) async-start(), calls=%async_computation.9 | async-start | bytes 2621440 | tf_op jit(solution)/shard_map/all_gather | solution.py:127
  13.2 48.2 %copy-start.11 = (f32[512,8]{0,1:T(8,128)}, f32[512,8]{0,1:T(8,128)S(1)}, u32[]{:S(2)}) copy-start(f32[512,8]{0,1:T(8,128)S(1)} %get-tuple-element.171) | copy-start | bytes 49156
  13.2 48.2 %copy-start.13 = (f32[512,8]{0,1:T(8,128)}, f32[512,8]{0,1:T(8,128)S(1)}, u32[]{:S(2)}) copy-start(f32[512,8]{0,1:T(8,128)S(1)} %get-tuple-element.172) | copy-start | bytes 49156
  31.9 29.2 %copy-start.15 = (f32[1,1024]{1,0:T(1,128)}, f32[1,1024]{1,0:T(1,128)S(1)}, u32[]{:S(2)}) copy-start(f32[1,1024]{1,0:T(1,128)S(1)} %get-tuple-element.161) | copy-start | bytes 12292
  31.9 29.2 %copy-start.19 = (f32[1,1024]{1,0:T(1,128)}, f32[1,1024]{1,0:T(1,128)S(1)}, u32[]{:S(2)}) copy-start(f32[1,1024]{1,0:T(1,128)S(1)} %get-tuple-element.162) | copy-start | bytes 12292
  61.1 2.1 copy-start.6
  61.3 1.1 copy-start.5
  61.3 6.1 copy-start.21
  61.3 24.2 %copy-start.1 = (f32[1,512,1024]{2,1,0:T(8,128)S(1)}, f32[1,512,1024]{2,1,0:T(8,128)}, u32[]{:S(2)}) copy-start(f32[1,512,1024]{2,1,0:T(8,128)} %param.31) | copy-start | bytes 6291460
  64.0 116.3 %all-gather.16.cloned.1.call-start = ((), (), s32[]{:S(2)}) async-start(), calls=%async_computation.8 | async-start | bytes 2621440 | tf_op jit(solution)/shard_map/all_gather | solution.py:128
  66.2 201.7 %all-gather.22.cloned.1.call-start = ((), (), s32[]{:S(2)}) async-start(), calls=%async_computation.11 | async-start | bytes 5242880 | tf_op jit(solution)/shard_map/all_gather | solution.py:99
  66.8 222.9 %all-gather.24.cloned.1.call-start = ((), (), s32[]{:S(2)}) async-start(), calls=%async_computation.12 | async-start | bytes 5242880 | tf_op jit(solution)/shard_map/all_gather | solution.py:100
  67.4 367.3 %reduce-scatter.12.cloned.1.call-start = ((), (), s32[]{:S(2)}) async-start(), calls=%async_computation.13 | async-start | bytes 10485760 | tf_op jit(solution)/shard_map/reduce_scatter | solution.py:214
  149.6 20.5 %copy-start = (f32[8,512,2048]{2,1,0:T(8,128)S(1)}, f32[8,512,2048]{2,1,0:T(8,128)}, u32[]{:S(2)}) copy-start(f32[8,512,2048]{2,1,0:T(8,128)} %get-tuple-element.176) | copy-start | bytes 100663296
  179.4 13.3 %copy-start.4 = (bf16[512,512]{0,1:T(8,128)(2,1)S(1)}, bf16[512,512]{0,1:T(8,128)(2,1)}, u32[]{:S(2)}) copy-start(bf16[512,512]{0,1:T(8,128)(2,1)} %fusion.75) | copy-start | bytes 1572868
  192.7 25.8 %copy-start.9 = (bf16[512,8,8]{0,2,1:T(8,128)(2,1)S(1)}, bf16[512,8,8]{0,2,1:T(8,128)(2,1)}, u32[]{:S(2)}) copy-start(bf16[512,8,8]{0,2,1:T(8,128)(2,1)} %get-tuple-element.147) | copy-start | bytes 196612
  192.7 25.8 %copy-start.10 = (bf16[512,8,8]{0,2,1:T(8,128)(2,1)S(1)}, bf16[512,8,8]{0,2,1:T(8,128)(2,1)}, u32[]{:S(2)}) copy-start(bf16[512,8,8]{0,2,1:T(8,128)(2,1)} %get-tuple-element.148) | copy-start | bytes 196612
  259.1 0.7 copy-start.23
  259.1 8.8 copy-start.3
  259.2 360.8 %reduce-scatter.20.cloned.1.call-start = ((), (), s32[]{:S(2)}) async-start(), calls=%async_computation.18 | async-start | bytes 8912896 | tf_op jit(solution)/shard_map/reduce_scatter | solution.py:259
  282.6 1.3 copy-start.8
  289.6 512.5 %reduce-scatter.18.cloned.1.call-start = ((), (), s32[]{:S(2)}) async-start(), calls=%async_computation.17 | async-start | bytes 8912896 | tf_op jit(solution)/shard_map/reduce_scatter | solution.py:258
  297.1 1.3 copy-start.32
  304.3 586.5 %reduce-scatter.16.cloned.1.call-start = ((), (), s32[]{:S(2)}) async-start(), calls=%async_computation.16 | async-start | bytes 2228224 | tf_op jit(solution)/shard_map/reduce_scatter | solution.py:257
  307.5 618.0 %all-reduce.4.cloned.1.call-start = ((), (), s32[]{:S(2)}) async-start(), calls=%async_computation.22 | async-start | bytes 12582912 | tf_op jit(solution)/shard_map/psum | solution.py:157
  307.9 6.6 copy-start.24
  307.9 6.6 copy-start.33
  337.1 104.4 %copy-start.12 = (f32[512,8]{0,1:T(8,128)S(1)}, f32[512,8]{0,1:T(8,128)}, u32[]{:S(2)}) copy-start(f32[512,8]{0,1:T(8,128)} %copy-done.11) | copy-start | bytes 49156
  337.1 104.4 %copy-start.14 = (f32[512,8]{0,1:T(8,128)S(1)}, f32[512,8]{0,1:T(8,128)}, u32[]{:S(2)}) copy-start(f32[512,8]{0,1:T(8,128)} %copy-done.13) | copy-start | bytes 49156
  456.6 0.7 copy-start.16
  456.6 0.7 copy-start.20
  456.6 610.5 %reduce-scatter.14.cloned.1.call-start = ((), (), s32[]{:S(2)}) async-start(), calls=%async_computation.14 | async-start | bytes 6684672 | tf_op jit(solution)/shard_map/reduce_scatter | solution.py:256
  463.9 360.8 %copy-start.31 = (u32[32]{0:T(128)S(1)}, u32[32]{0:T(128)}, u32[]{:S(2)}) copy-start(u32[32]{0:T(128)} %constant.168) | copy-start | bytes 388
  463.9 679.0 %reduce-scatter.24.cloned.1.call-start = ((), (), s32[]{:S(2)}) async-start(), calls=%async_computation.21 | async-start | bytes 278528
  466.9 719.8 %all-gather.28.cloned.1.call-start = ((), (), s32[]{:S(2)}) async-start(), calls=%async_computation.19 | async-start | bytes 2621440 | tf_op jit(solution)/shard_map/all_gather | solution.py:286
  620.0 645.0 %reduce-scatter.22.cloned.1.call-start = ((), (), s32[]{:S(2)}) async-start(), calls=%async_computation.20 | async-start | bytes 557056
  802.1 22.4 %collective-permute-start = (f32[64,2048]{1,0:T(8,128)}, f32[64,2048]{1,0:T(8,128)}, u32[]{:S(2)}, u32[]{:S(2)}) collective-permute-start(f32[64,2048]{1,0:T(8,128)} %reduce-scatter.18.cloned.1.call-done), channel_id=1, source_target_pairs={{0,2},{2,4},{4,6},{6,0},{1,3},{3,5},{5,7},{7,1},{8,10},{10,12},{12... | collective-permute-start | bytes 1572872 | tf_op jit(solution)/shard_map/ppermute | solution.py:271
  824.5 87.4 %collective-permute-start.1 = (f32[64,2048]{1,0:T(8,128)}, f32[64,2048]{1,0:T(8,128)}, u32[]{:S(2)}, u32[]{:S(2)}) collective-permute-start(f32[64,2048]{1,0:T(8,128)} %collective-permute-done), channel_id=1, source_target_pairs={{0,2},{2,4},{4,6},{6,0},{1,3},{3,5},{5,7},{7,1},{8,10},{10,12},{12... | collective-permute-start | bytes 1572872 | tf_op jit(solution)/shard_map/ppermute | solution.py:271
  909.9 9.4 collective-permute-start.2
  919.3 0.8 copy-start.7
  930.0 370.1 %all-gather.26.cloned.1.call-start = ((), (), s32[]{:S(2)}) async-start(), calls=%async_computation.15 | async-start | bytes 1966080 | tf_op jit(solution)/shard_map/all_gather | solution.py:283
  1070.9 118.7 %copy-start.17 = (f32[1,1024]{1,0:T(1,128)S(1)}, f32[1,1024]{1,0:T(1,128)}, u32[]{:S(2)}) copy-start(f32[1,1024]{1,0:T(1,128)} %get-tuple-element.159) | copy-start | bytes 12292
  1070.9 118.7 %copy-start.18 = (f32[1,1024]{1,0:T(1,128)S(1)}, f32[1,1024]{1,0:T(1,128)}, u32[]{:S(2)}) copy-start(f32[1,1024]{1,0:T(1,128)} %get-tuple-element.160) | copy-start | bytes 12292
Sparse Core Ops, SparseCore 0:
  10.5 46.6 all-gather.13
  59.0 26.4 all-gather.19
  87.7 45.9 all-gather.17
  135.6 44.6 all-gather.15
  182.0 51.4 all-gather.21
  235.1 52.6 all-gather.23
  290.1 144.4 reduce-scatter.11
  436.9 183.0 reduce-scatter.19
  622.3 179.8 reduce-scatter.17
  804.8 85.8 reduce-scatter.15
  894.7 30.7 all-reduce.3
  927.7 139.3 reduce-scatter.13
  1069.5 73.3 reduce-scatter.23
  1144.3 42.3 all-gather.27
  1189.4 75.6 reduce-scatter.21
  1266.6 33.4 all-gather.25
